TPU v7x, 512 devices: a whole 4x8x8 slice. The times are simulated.
512 devices in a mesh: dp: 32 (over x_lo, y, core), head: 16 (over z, x_hi).
Axes of the slice: x: 4 (x_hi: 2, x_lo: 2; x = x_hi * 2 + x_lo), y: 8, z: 8, core: 2. Of those that a mesh axis runs over, the one named last changes fastest.
Arguments:
- hidden_in: bfloat16 [8192, 7168], P('dp', 'head'), may hold values from -6 to 6
- latent_unnormed: bfloat16 [8192, 512], P('dp'), may hold values from -6 to 6
- unrotated_key: bfloat16 [8192, 64], P('dp'), may hold values from -6 to 6
- latent_norm_scale: float32 [512], replicated, may hold values from 0.1 to 1.9
- plain_query_rows: bfloat16 [8192, 16384], P('dp', 'head'), may hold values from -6 to 6
- rotated_query_rows: bfloat16 [8192, 8192], P('dp', 'head'), may hold values from -240 to 240
- key_up_matrix: bfloat16 [512, 16384], P('dp', 'head'), may hold values from -0.25 to 0.25
- value_up_matrix: bfloat16 [512, 16384], P('dp', 'head'), may hold values from -0.25 to 0.25
- output_cotangent: bfloat16 [8192, 16384], P('dp', 'head'), may hold values from -6 to 6
- down_weight: float32 [576, 7168], P('dp', 'head'), may hold values from -0.0625 to 0.0625
- first_moment: float32 [576, 7168], P('dp', 'head'), may hold values from -0.078125 to 0.078125
- second_moment: float32 [576, 7168], P('dp', 'head'), may hold values from 4e-08 to 4e-07
Outputs:
- query_grad_nope: bfloat16 [8192, 16384], P('dp', 'head')
- query_grad_rope: bfloat16 [8192, 8192], P('dp', 'head')
- new_weight: float32 [576, 7168], P('dp', 'head')
- new_first: float32 [576, 7168], P('dp', 'head')
- new_second: float32 [576, 7168], P('dp', 'head')
All inputs are finite; a program needn't handle non-finite values.
Results may differ from a plain program's by a relative error of at most 0.011.
The roundings to bfloat16 on the way count: a program that leaves them out, or rounds other values in their place, can miss the bound.
Values may be sent and summed in bfloat16 or wider, within the bound.
A program may use at most 64 MiB of HBM per device.

v0:
```python
import math
import jax
import jax.numpy as jnp
from jax import lax
from jax.sharding import PartitionSpec as P

SEQUENCE_LENGTH = 256
norm_eps = 1e-06
beta_one = 0.9
beta_two = 0.999
adam_eps = 1e-08
learn_rate = 0.01
decay_rate = 0.1
bias_one = 1.0 - 0.9**2
bias_two = 1.0 - 0.999**2


def angle_tables(positions, rope_width):
    half_width = rope_width // 2
    inverse_freq = jnp.exp(
        jnp.arange(half_width, dtype=jnp.float32) * (-2.0 * math.log(10000.0) / rope_width)
    )
    angles = positions.astype(jnp.float32)[:, None] * inverse_freq[None, :]
    return (jnp.cos(angles), jnp.sin(angles))


def latent_back(
    latent_sum, rope_sum, latent_in, inverse_rms, latent_norm_scale, cos_table, sin_table
):
    latent_width = latent_in.shape[1]
    scaled_grad = latent_norm_scale * latent_sum
    inner_sum = jnp.sum(latent_in * scaled_grad, axis=1, keepdims=True)
    latent_grad = (
        inverse_rms * scaled_grad
        - latent_in * (inverse_rms * inverse_rms * inverse_rms) * inner_sum / latent_width
    )
    half_width = rope_sum.shape[1] // 2
    grad_first = rope_sum[:, :half_width]
    grad_second = rope_sum[:, half_width:]
    rope_grad = jnp.concatenate(
        (
            grad_first * cos_table + grad_second * sin_table,
            grad_second * cos_table - grad_first * sin_table,
        ),
        axis=1,
    )
    return jnp.concatenate((latent_grad, rope_grad), axis=1).astype(jnp.bfloat16)


def local(
    hidden_in,
    latent_unnormed,
    unrotated_key,
    latent_norm_scale,
    plain_query_rows,
    rotated_query_rows,
    key_up_matrix,
    value_up_matrix,
    output_cotangent,
    down_weight,
    first_moment,
    second_moment,
):
    row_count = latent_unnormed.shape[0]
    rope_width = unrotated_key.shape[1]
    head_count = rotated_query_rows.shape[1] // rope_width
    nope_width = plain_query_rows.shape[1] // head_count
    value_width = output_cotangent.shape[1] // head_count
    seq_count = row_count // SEQUENCE_LENGTH
    scale_factor = 1.0 / math.sqrt(nope_width + rope_width)
    positions = jnp.arange(row_count, dtype=jnp.int32) % SEQUENCE_LENGTH
    cos_table, sin_table = angle_tables(positions, rope_width)
    raw_key = unrotated_key.astype(jnp.float32)
    half_width = rope_width // 2
    first_half = raw_key[:, :half_width]
    second_half = raw_key[:, half_width:]
    key_rot = jnp.concatenate(
        (
            first_half * cos_table - second_half * sin_table,
            first_half * sin_table + second_half * cos_table,
        ),
        axis=1,
    ).astype(jnp.bfloat16)
    latent_in = latent_unnormed.astype(jnp.float32)
    inverse_rms = lax.rsqrt(jnp.mean(latent_in * latent_in, axis=1, keepdims=True) + norm_eps)
    latent = (latent_in * inverse_rms * latent_norm_scale).astype(jnp.bfloat16)
    joined = jnp.concatenate((key_up_matrix, value_up_matrix), axis=1)
    split_at = head_count * nope_width
    full_rows = lax.all_gather(joined, "dp", axis=0, tiled=True)
    projected = jnp.dot(latent, full_rows, preferred_element_type=jnp.float32)
    key_nope = (
        projected[:, :split_at]
        .astype(jnp.bfloat16)
        .reshape(seq_count, SEQUENCE_LENGTH, head_count, nope_width)
    )
    value_rows = (
        projected[:, split_at:]
        .astype(jnp.bfloat16)
        .reshape(seq_count, SEQUENCE_LENGTH, head_count, value_width)
    )
    nope_query = plain_query_rows.reshape(seq_count, SEQUENCE_LENGTH, head_count, nope_width)
    rope_query = rotated_query_rows.reshape(seq_count, SEQUENCE_LENGTH, head_count, rope_width)
    grad_rows = output_cotangent.reshape(seq_count, SEQUENCE_LENGTH, head_count, value_width)
    rot_rows = key_rot.reshape(seq_count, SEQUENCE_LENGTH, rope_width)
    scores = (
        jnp.einsum("bthd,bshd->bhts", nope_query, key_nope, preferred_element_type=jnp.float32)
        + jnp.einsum("bthd,bsd->bhts", rope_query, rot_rows, preferred_element_type=jnp.float32)
    ) * scale_factor
    causal = jnp.arange(SEQUENCE_LENGTH)[:, None] >= jnp.arange(SEQUENCE_LENGTH)[None, :]
    scores = jnp.where(causal, scores, -1e30)
    maxima = jnp.max(scores, axis=-1, keepdims=True)
    exponent = jnp.exp(scores - maxima)
    probabilities = exponent / jnp.sum(exponent, axis=-1, keepdims=True)
    prob_low = probabilities.astype(jnp.bfloat16)
    attended = jnp.einsum(
        "bhts,bshd->bthd", prob_low, value_rows, preferred_element_type=jnp.float32
    )
    delta_sum = jnp.einsum("bthd,bthd->bht", grad_rows.astype(jnp.float32), attended)
    grad_probs = jnp.einsum(
        "bthd,bshd->bhts", grad_rows, value_rows, preferred_element_type=jnp.float32
    )
    grad_scores = probabilities * (grad_probs - delta_sum[..., None]) * scale_factor
    score_low = grad_scores.astype(jnp.bfloat16)
    grad_nope_q = jnp.einsum(
        "bhts,bshd->bthd", score_low, key_nope, preferred_element_type=jnp.float32
    ).astype(jnp.bfloat16)
    grad_rope_q = jnp.einsum(
        "bhts,bsd->bthd", score_low, rot_rows, preferred_element_type=jnp.float32
    ).astype(jnp.bfloat16)
    grad_key = jnp.einsum(
        "bhts,bthd->bshd", score_low, nope_query, preferred_element_type=jnp.float32
    ).astype(jnp.bfloat16)
    grad_value = jnp.einsum(
        "bhts,bthd->bshd", prob_low, grad_rows, preferred_element_type=jnp.float32
    ).astype(jnp.bfloat16)
    rope_part = jnp.einsum(
        "bhts,bthd->bsd", score_low, rope_query, preferred_element_type=jnp.float32
    ).reshape(row_count, rope_width)
    grads_joined = jnp.concatenate(
        (
            grad_key.reshape(row_count, split_at),
            grad_value.reshape(row_count, head_count * value_width),
        ),
        axis=1,
    )
    latent_part = jnp.einsum(
        "tk,ck->tc", grads_joined, full_rows, preferred_element_type=jnp.float32
    )
    latent_sum, rope_sum = lax.psum((latent_part, rope_part), "head")
    kv_grad = latent_back(
        latent_sum, rope_sum, latent_in, inverse_rms, latent_norm_scale, cos_table, sin_table
    )
    weight_sum = lax.psum_scatter(
        jnp.einsum("tc,td->cd", kv_grad, hidden_in, preferred_element_type=jnp.float32),
        "dp",
        scatter_dimension=0,
        tiled=True,
    )
    weight_grad = weight_sum / (row_count * lax.axis_size("dp"))
    new_first = beta_one * first_moment + (1.0 - beta_one) * weight_grad
    new_second = beta_two * second_moment + (1.0 - beta_two) * weight_grad * weight_grad
    direction = new_first / bias_one / (jnp.sqrt(new_second / bias_two) + adam_eps)
    new_weight = down_weight - learn_rate * (direction + decay_rate * down_weight)
    return (
        grad_nope_q.reshape(row_count, split_at),
        grad_rope_q.reshape(row_count, head_count * rope_width),
        new_weight,
        new_first,
        new_second,
    )


def solution(mesh):
    placed = (
        P("dp", "head"),
        P("dp", None),
        P("dp", None),
        P(),
        P("dp", "head"),
        P("dp", "head"),
        P("dp", "head"),
        P("dp", "head"),
        P("dp", "head"),
        P("dp", "head"),
        P("dp", "head"),
        P("dp", "head"),
    )
    return jax.shard_map(
        local,
        mesh=mesh,
        in_specs=placed,
        out_specs=(
            P("dp", "head"),
            P("dp", "head"),
            P("dp", "head"),
            P("dp", "head"),
            P("dp", "head"),
        ),
        check_vma=False,
    )
```

profile of v0, /device:TPU:48, one launch (start us, length us, event | category | flops | bytes accessed | tf_op | source)
XLA Modules:
  0.0 377.6 jit_solution(13306628696366333491)
XLA Ops:
  7.2 1.5 pad_maximum_fusion
  8.8 1.2 copy.89
  10.1 0.8 convert_element_type.88
  10.9 1.8 copy.58
  12.8 1.2 copy.69
  14.1 0.6 multiply_multiply_fusion
  14.9 65.6 %all-gather.2.cloned.1.call-done = bf16[512,2048]{1,0:T(8,128)(2,1)} async-done(((bf16[16,2048]{1,0:T(8,128)(2,1)}), bf16[512,2048]{1,0:T(8,128)(2,1)}) %all-gather.2.cloned.1.call-update) | async-done | bytes 2097168 | tf_op jit(solution)/shard_map/all_gather | solution.py:89
  80.5 2.4 convolution_convert_fusion
  82.9 0.9 fusion.53
  84.0 0.5 fusion.55
  84.5 0.6 copy-done.8
  85.2 0.6 fusion.54
  86.1 0.3 fusion.14
  86.4 2.1 copy.90
  88.4 2.3 convolution_bitcast_fusion
  90.8 2.6 copy.81
  93.3 1.7 multiply_reduce_fusion
  95.0 0.7 copy.82
  95.7 1.6 convolution_convert_fusion.1
  97.4 0.7 fusion.7
  98.1 0.3 copy-done.5
  98.4 0.5 convolution_convert_fusion.2
  98.9 0.5 copy-done.9
  99.3 1.1 convolution_bitcast_fusion.1
  100.5 1.6 fusion.8
  102.1 1.3 dynamic-slice.4
  104.0 164.9 %all-reduce.5.cloned.1.call-done = (f32[256,64]{0,1:T(8,128)}, f32[256,512]{1,0:T(8,128)}) async-done(((f32[256,64]{0,1:T(8,128)}, f32[256,512]{1,0:T(8,128)}), (f32[256,64]{0,1:T(8,128)}, f32[256,512]{1,0:T(8,128)})) %all-reduce.5.cloned.1.call-update) | async-done | bytes 589840 | tf_op jit(solution)/shard_map/psum | solution.py:149
  268.8 1.2 fusion.22
  270.0 1.0 fusion.45
  271.3 1.3 fusion.21
  272.6 0.4 fusion.23
  273.0 54.6 %fusion = f32[24,448]{1,0:T(8,128)S(1)} fusion(f32[576,448]{1,0:T(8,128)S(1)} %fusion.23), kind=kCustom, calls=%all-reduce-scatter | all-reduce-scatter fusion | flops 344065 | bytes 1077248
  327.6 4.2 %collective-permute-start = (f32[24,448]{1,0:T(8,128)S(1)}, f32[24,448]{1,0:T(8,128)S(1)}, u32[]{:S(2)}, u32[]{:S(2)}) collective-permute-start(f32[24,448]{1,0:T(8,128)S(1)} %fusion), channel_id=1, source_target_pairs={{0,16},{16,32},{32,48},{48,64},{64,80},{80,96},{96,112},{112,128},... | collective-permute-start | bytes 129032
  331.8 6.7 %collective-permute-start.1 = (f32[24,448]{1,0:T(8,128)S(1)}, f32[24,448]{1,0:T(8,128)S(1)}, u32[]{:S(2)}, u32[]{:S(2)}) collective-permute-start(f32[24,448]{1,0:T(8,128)S(1)} %fusion), channel_id=1, source_target_pairs={{0,32},{16,48},{32,64},{48,80},{64,96},{80,112},{96,128},{112,144}... | collective-permute-start | bytes 129032
  338.5 1.9 collective-permute-start.7
  340.4 0.3 convolution_convert_fusion.3
  340.8 6.1 %collective-permute-start.2 = (f32[24,448]{1,0:T(8,128)S(1)}, f32[24,448]{1,0:T(8,128)S(1)}, u32[]{:S(2)}, u32[]{:S(2)}) collective-permute-start(f32[24,448]{1,0:T(8,128)S(1)} %fusion), channel_id=1, source_target_pairs={{0,48},{16,64},{32,80},{48,96},{64,112},{80,128},{96,144},{112,160... | collective-permute-start | bytes 129032
  346.9 2.2 collective-permute-start.3
  349.0 4.5 %collective-permute-start.4 = (f32[24,448]{1,0:T(8,128)S(1)}, f32[24,448]{1,0:T(8,128)S(1)}, u32[]{:S(2)}, u32[]{:S(2)}) collective-permute-start(f32[24,448]{1,0:T(8,128)S(1)} %fusion), channel_id=1, source_target_pairs={{0,80},{16,96},{32,112},{48,128},{64,144},{80,160},{96,176},{112,1... | collective-permute-start | bytes 129032
  353.5 2.7 collective-permute-start.5
  356.3 3.2 collective-permute-start.6
  359.5 0.3 convolution_convert_fusion.4
  359.8 1.0 copy.73
  360.8 0.8 copy.74
  361.7 0.9 collective-permute-done.5
  362.5 6.4 %collective-permute-done.6 = f32[24,448]{1,0:T(8,128)S(1)} collective-permute-done((f32[24,448]{1,0:T(8,128)S(1)}, f32[24,448]{1,0:T(8,128)S(1)}, u32[]{:S(2)}, u32[]{:S(2)}) %collective-permute-start.6) | collective-permute-done | bytes 43040
  368.9 1.1 concatenate.21
  370.0 0.7 multiply_subtract_fusion
  (72 shorter events, 1.5 us)
Async XLA Ops:
  7.2 265.4 %copy-start = (bf16[256,448]{0,1:T(8,128)(2,1)S(1)}, bf16[256,448]{0,1:T(8,128)(2,1)}, u32[]{:S(2)}) copy-start(bf16[256,448]{0,1:T(8,128)(2,1)} %param.12) | copy-start | bytes 688132
  7.2 5.5 %copy-start.13 = (bf16[256,1024]{1,0:T(8,128)(2,1)S(1)}, bf16[256,1024]{1,0:T(8,128)(2,1)}, u32[]{:S(2)}) copy-start(bf16[256,1024]{1,0:T(8,128)(2,1)} %param.20) | copy-start | bytes 1572868
  7.2 6.8 %copy-start.6 = (bf16[256,512]{1,0:T(8,128)(2,1)S(1)}, bf16[256,512]{1,0:T(8,128)(2,1)}, u32[]{:S(2)}) copy-start(bf16[256,512]{1,0:T(8,128)(2,1)} %param.13) | copy-start | bytes 786436
  7.2 73.3 %all-gather.2.cloned.1.call-start = ((), (), s32[]{:S(2)}) async-start(), calls=%async_computation | async-start | bytes 2162688 | tf_op jit(solution)/shard_map/all_gather | solution.py:89
  8.8 71.8 %copy-start.17 = (f32[512]{0:T(512)S(1)}, f32[512]{0:T(512)}, u32[]{:S(2)}) copy-start(f32[512]{0:T(512)} %param.15) | copy-start | bytes 6148
  8.8 260.1 %all-reduce.5.cloned.1.call-start = ((), (), s32[]{:S(2)}) async-start(), calls=%async_computation.1 | async-start | bytes 1179648 | tf_op jit(solution)/shard_map/psum | solution.py:149
  10.1 74.0 %copy-start.4 = (bf16[256,1024]{0,1:T(8,128)(2,1)}, bf16[256,1024]{0,1:T(8,128)(2,1)S(1)}, u32[]{:S(2)}) copy-start(bf16[256,1024]{0,1:T(8,128)(2,1)S(1)} %copy.89) | copy-start | bytes 1572868
  12.8 70.1 %copy-start.1 = (bf16[32,8,8,128]{3,2,1,0:T(8,128)(2,1)}, bf16[32,8,8,128]{3,2,1,0:T(8,128)(2,1)S(1)}, u32[]{:S(2)}) copy-start(bf16[32,8,8,128]{3,2,1,0:T(8,128)(2,1)S(1)} %copy.91) | copy-start | bytes 1572868
  13.9 69.9 %copy-start.25 = (f32[32]{0:T(128)}, f32[32]{0:T(128)S(1)}, u32[]{:S(2)}) copy-start(f32[32]{0:T(128)S(1)} %multiply_exponential_fusion) | copy-start | bytes 388
  13.9 69.8 %copy-start.22 = (f32[256]{0:T(256)}, f32[256]{0:T(256)S(1)}, u32[]{:S(2)}) copy-start(f32[256]{0:T(256)S(1)} %fusion.48) | copy-start | bytes 3076
  14.7 69.1 %copy-start.19 = (f32[256]{0:T(256)}, f32[256]{0:T(256)S(1)}, u32[]{:S(2)}) copy-start(f32[256]{0:T(256)S(1)} %get-tuple-element.32) | copy-start | bytes 3076
  84.0 1.7 copy-start.2
  84.0 1.1 copy-start.8
  95.7 1.6 copy-start.10
  95.7 1.6 copy-start.12
  95.7 1.6 copy-start.21
  97.3 1.0 copy-start.5
  98.4 0.9 copy-start.9
  98.4 2.0 copy-start.11
  100.4 168.4 %copy-start.7 = (bf16[256,512]{1,0:T(8,128)(2,1)S(1)}, bf16[256,512]{1,0:T(8,128)(2,1)}, u32[]{:S(2)}) copy-start(bf16[256,512]{1,0:T(8,128)(2,1)} %param.13) | copy-start | bytes 786436
  100.4 168.4 %copy-start.18 = (f32[512]{0:T(512)S(1)}, f32[512]{0:T(512)}, u32[]{:S(2)}) copy-start(f32[512]{0:T(512)} %param.15) | copy-start | bytes 6148
  100.4 169.6 %copy-start.23 = (f32[256]{0:T(256)S(1)}, f32[256]{0:T(256)}, u32[]{:S(2)}) copy-start(f32[256]{0:T(256)} %copy-done.22) | copy-start | bytes 3076
  100.4 169.6 %copy-start.26 = (f32[32]{0:T(128)S(1)}, f32[32]{0:T(128)}, u32[]{:S(2)}) copy-start(f32[32]{0:T(128)} %copy-done.25) | copy-start | bytes 388
  100.4 170.8 %copy-start.20 = (f32[256]{0:T(256)S(1)}, f32[256]{0:T(256)}, u32[]{:S(2)}) copy-start(f32[256]{0:T(256)} %copy-done.19) | copy-start | bytes 3076
  100.5 170.8 %copy-start.24 = (f32[256]{0:T(256)S(1)}, f32[256]{0:T(256)}, u32[]{:S(2)}) copy-start(f32[256]{0:T(256)} %get-tuple-element.31) | copy-start | bytes 3076
  271.3 69.1 %copy-start.3 = (bf16[256,1024]{0,1:T(8,128)(2,1)S(1)}, bf16[256,1024]{0,1:T(8,128)(2,1)}, u32[]{:S(2)}) copy-start(bf16[256,1024]{0,1:T(8,128)(2,1)} %copy-done.2) | copy-start | bytes 1572868
  327.6 25.9 %collective-permute-start = (f32[24,448]{1,0:T(8,128)S(1)}, f32[24,448]{1,0:T(8,128)S(1)}, u32[]{:S(2)}, u32[]{:S(2)}) collective-permute-start(f32[24,448]{1,0:T(8,128)S(1)} %fusion), channel_id=1, source_target_pairs={{0,16},{16,32},{32,48},{48,64},{64,80},{80,96},{96,112},{112,128},... | collective-permute-start | bytes 129032
  331.8 24.5 %collective-permute-start.1 = (f32[24,448]{1,0:T(8,128)S(1)}, f32[24,448]{1,0:T(8,128)S(1)}, u32[]{:S(2)}, u32[]{:S(2)}) collective-permute-start(f32[24,448]{1,0:T(8,128)S(1)} %fusion), channel_id=1, source_target_pairs={{0,32},{16,48},{32,64},{48,80},{64,96},{80,112},{96,128},{112,144}... | collective-permute-start | bytes 129032
  338.5 10.6 %collective-permute-start.7 = (f32[18,448]{1,0:T(8,128)S(1)}, f32[18,448]{1,0:T(8,128)S(1)}, u32[]{:S(2)}, u32[]{:S(2)}) collective-permute-start(f32[18,448]{1,0:T(8,128)S(1)} %slice.32), channel_id=1, source_target_pairs={{0,128},{16,144},{32,160},{48,176},{64,192},{80,208},{96,224},{112... | collective-permute-start | bytes 96776
  340.7 29.3 %copy-start.14 = (f32[18,448]{1,0:T(8,128)S(1)}, f32[18,448]{1,0:T(8,128)}, u32[]{:S(2)}) copy-start(f32[18,448]{1,0:T(8,128)} %param.21) | copy-start | bytes 96772
  340.7 29.3 %copy-start.15 = (f32[18,448]{1,0:T(8,128)S(1)}, f32[18,448]{1,0:T(8,128)}, u32[]{:S(2)}) copy-start(f32[18,448]{1,0:T(8,128)} %param.22) | copy-start | bytes 96772
  340.7 29.3 %copy-start.16 = (f32[18,448]{1,0:T(8,128)S(1)}, f32[18,448]{1,0:T(8,128)}, u32[]{:S(2)}) copy-start(f32[18,448]{1,0:T(8,128)} %param.23) | copy-start | bytes 96772
  340.8 20.9 %collective-permute-start.2 = (f32[24,448]{1,0:T(8,128)S(1)}, f32[24,448]{1,0:T(8,128)S(1)}, u32[]{:S(2)}, u32[]{:S(2)}) collective-permute-start(f32[24,448]{1,0:T(8,128)S(1)} %fusion), channel_id=1, source_target_pairs={{0,48},{16,64},{32,80},{48,96},{64,112},{80,128},{96,144},{112,160... | collective-permute-start | bytes 129032
  346.9 14.8 %collective-permute-start.3 = (f32[24,448]{1,0:T(8,128)S(1)}, f32[24,448]{1,0:T(8,128)S(1)}, u32[]{:S(2)}, u32[]{:S(2)}) collective-permute-start(f32[24,448]{1,0:T(8,128)S(1)} %fusion), channel_id=1, source_target_pairs={{0,64},{16,80},{32,96},{48,112},{64,128},{80,144},{96,160},{112,17... | collective-permute-start | bytes 129032
  349.0 12.7 %collective-permute-start.4 = (f32[24,448]{1,0:T(8,128)S(1)}, f32[24,448]{1,0:T(8,128)S(1)}, u32[]{:S(2)}, u32[]{:S(2)}) collective-permute-start(f32[24,448]{1,0:T(8,128)S(1)} %fusion), channel_id=1, source_target_pairs={{0,80},{16,96},{32,112},{48,128},{64,144},{80,160},{96,176},{112,1... | collective-permute-start | bytes 129032
  353.5 9.0 %collective-permute-start.5 = (f32[24,448]{1,0:T(8,128)S(1)}, f32[24,448]{1,0:T(8,128)S(1)}, u32[]{:S(2)}, u32[]{:S(2)}) collective-permute-start(f32[24,448]{1,0:T(8,128)S(1)} %fusion), channel_id=1, source_target_pairs={{0,96},{16,112},{32,128},{48,144},{64,160},{80,176},{96,192},{112,... | collective-permute-start | bytes 129032
  356.3 12.6 %collective-permute-start.6 = (f32[24,448]{1,0:T(8,128)S(1)}, f32[24,448]{1,0:T(8,128)S(1)}, u32[]{:S(2)}, u32[]{:S(2)}) collective-permute-start(f32[24,448]{1,0:T(8,128)S(1)} %fusion), channel_id=1, source_target_pairs={{0,112},{16,128},{32,144},{48,160},{64,176},{80,192},{96,208},{112... | collective-permute-start | bytes 129032
Sparse Core Ops, SparseCore 0:
  10.8 69.7 all-gather.1
  102.2 166.6 all-reduce.4
where the time goes:
time: 379 us; the launch traced here: 378 us
  waiting for transfers between devices  238 us (63%)
  blocking collectives  54.6 us (14%)
  starting transfers between devices  31.6 us (8%)
  local copies, waits for them, and re-layouts  16.6 us (4%)
  between operations  15.2 us (4%)
  matrix products  12.2 us (3%)
  other arithmetic  9.68 us (3%)
    psum x1, waiting for transfers between devices, local(): latent_sum, rope_sum = lax.psum((latent_part, rope_part), 'head')  165 us
    all_gather x1, waiting for transfers between devices, local(): full_rows = lax.all_gather(joined, 'dp', axis=0, tiled=True)  65.6 us
    unnamed x1, blocking collectives  54.6 us
    unnamed x8, starting transfers between devices  31.5 us
    unnamed x62, local copies, waits for them, and re-layouts  10.2 us
  transfers between devices with their start and end apart: 10, of which 4 were waited for; matrix products, arithmetic and copies ran while one was open for 3% of the time, Pallas kernels for 0%

commit v1 on v0

--- a/solution.py
+++ b/solution.py
@@ -86,7 +86,9 @@
     latent = (latent_in * inverse_rms * latent_norm_scale).astype(jnp.bfloat16)
     joined = jnp.concatenate((key_up_matrix, value_up_matrix), axis=1)
     split_at = head_count * nope_width
-    full_rows = lax.all_gather(joined, "dp", axis=0, tiled=True)
+    full_rows = jnp.concatenate(
+        lax.all_to_all(jnp.stack([joined] * lax.axis_size("dp")), "dp", 0, 0), axis=0
+    )
     projected = jnp.dot(latent, full_rows, preferred_element_type=jnp.float32)
     key_nope = (
         projected[:, :split_at]

time: 379 us -> 366 us (0.966)
  waiting for transfers between devices: 238 us -> 215 us
  starting transfers between devices: 31.6 us -> 40.7 us
    all_gather x1 -> x0, waiting for transfers between devices: 65.6 us -> none  [local(): full_rows = lax.all_gather(joined, 'dp', axis=0, tiled=True)]
    all_to_all x0 -> x1, waiting for transfers between devices: none -> 41.4 us  [local(): lax.all_to_all(jnp.stack([joined] * lax.axis_size('dp')), 'dp', 0, 0)]
    all_to_all x0 -> x1, starting transfers between devices: none -> 9.13 us  [local(): lax.all_to_all(jnp.stack([joined] * lax.axis_size('dp')), 'dp', 0, 0)]
    unnamed x62 -> x64, local copies, waits for them, and re-layouts: 10.2 us -> 11 us
where the time goes in v1:
time: 366 us; the launch traced here: 365 us
  waiting for transfers between devices  215 us (59%)
  blocking collectives  54.6 us (15%)
  starting transfers between devices  40.7 us (11%)
  local copies, waits for them, and re-layouts  19.2 us (5%)
  between operations  15.2 us (4%)
  matrix products  11.7 us (3%)
  other arithmetic  9.19 us (3%)
    psum x1, waiting for transfers between devices, local(): latent_sum, rope_sum = lax.psum((latent_part, rope_part), 'head')  166 us
    unnamed x1, blocking collectives  54.6 us
    all_to_all x1, waiting for transfers between devices, local(): lax.all_to_all(jnp.stack([joined] * lax.axis_size('dp')), 'dp', 0, 0)  41.4 us
    unnamed x8, starting transfers between devices  31.5 us
    unnamed x64, local copies, waits for them, and re-layouts  11 us
    all_to_all x1, starting transfers between devices, local(): lax.all_to_all(jnp.stack([joined] * lax.axis_size('dp')), 'dp', 0, 0)  9.13 us
  transfers between devices with their start and end apart: 10, of which 4 were waited for; matrix products, arithmetic and copies ran while one was open for 3% of the time, Pallas kernels for 0%

profile of v1, /device:TPU:48, one launch (start us, length us, event | category | flops | bytes accessed | tf_op | source)
XLA Modules:
  0.0 365.3 jit_solution(2515973657941563254)
XLA Ops:
  7.2 0.8 pad_maximum_fusion
  8.0 1.6 stack.2
  9.6 9.1 %all-to-all-start = ((bf16[32,16,2048]{2,1,0:T(8,128)(2,1)}), bf16[32,16,2048]{2,1,0:T(8,128)(2,1)S(1)}, u32[]{:S(2)}, u32[]{:S(2)}) async-start(bf16[32,16,2048]{2,1,0:T(8,128)(2,1)} %stack.2), calls=%async_computation | async-start | bytes 4194304 | tf_op jit(solution)/shard_map/all_to_all | solution.py:90
  19.1 2.0 copy.58
  21.0 1.1 copy.91
  22.2 1.2 copy.69
  23.4 1.1 fusion.15
  24.5 0.6 multiply_multiply_fusion
  25.3 41.4 %all-to-all-done = bf16[32,16,2048]{2,1,0:T(8,128)(2,1)S(1)} async-done(((bf16[32,16,2048]{2,1,0:T(8,128)(2,1)}), bf16[32,16,2048]{2,1,0:T(8,128)(2,1)S(1)}, u32[]{:S(2)}, u32[]{:S(2)}) %all-to-all-start) | async-done | bytes 2097184 | tf_op jit(solution)/shard_map/all_to_all | solution.py:90
  66.7 1.9 convolution_convert_fusion
  68.5 1.1 fusion.53
  69.6 1.2 copy.88
  70.9 0.5 fusion.55
  71.4 0.6 copy-done.9
  72.0 0.6 fusion.54
  72.9 0.3 fusion.14
  73.2 2.1 copy.90
  75.3 2.3 convolution_bitcast_fusion
  77.6 2.6 copy.81
  80.2 1.7 multiply_reduce_fusion
  81.9 0.7 copy.82
  82.5 1.6 convolution_convert_fusion.1
  84.2 0.7 fusion.7
  85.2 0.5 convolution_convert_fusion.2
  85.7 1.1 convolution_bitcast_fusion.1
  86.9 1.6 fusion.8
  88.5 1.3 dynamic-slice.4
  90.4 166.2 %all-reduce.5.cloned.1.call-done = (f32[256,64]{0,1:T(8,128)}, f32[256,512]{1,0:T(8,128)}) async-done(((f32[256,64]{0,1:T(8,128)}, f32[256,512]{1,0:T(8,128)}), (f32[256,64]{0,1:T(8,128)}, f32[256,512]{1,0:T(8,128)})) %all-reduce.5.cloned.1.call-update) | async-done | bytes 589840 | tf_op jit(solution)/shard_map/psum | solution.py:151
  256.6 1.2 fusion.22
  257.8 1.0 fusion.45
  259.0 1.3 fusion.21
  260.3 0.4 fusion.23
  260.7 54.6 %fusion = f32[24,448]{1,0:T(8,128)S(1)} fusion(f32[576,448]{1,0:T(8,128)S(1)} %fusion.23), kind=kCustom, calls=%all-reduce-scatter | all-reduce-scatter fusion | flops 344065 | bytes 1077248
  315.3 4.2 %collective-permute-start = (f32[24,448]{1,0:T(8,128)S(1)}, f32[24,448]{1,0:T(8,128)S(1)}, u32[]{:S(2)}, u32[]{:S(2)}) collective-permute-start(f32[24,448]{1,0:T(8,128)S(1)} %fusion), channel_id=1, source_target_pairs={{0,16},{16,32},{32,48},{48,64},{64,80},{80,96},{96,112},{112,128},... | collective-permute-start | bytes 129032
  319.5 6.7 %collective-permute-start.1 = (f32[24,448]{1,0:T(8,128)S(1)}, f32[24,448]{1,0:T(8,128)S(1)}, u32[]{:S(2)}, u32[]{:S(2)}) collective-permute-start(f32[24,448]{1,0:T(8,128)S(1)} %fusion), channel_id=1, source_target_pairs={{0,32},{16,48},{32,64},{48,80},{64,96},{80,112},{96,128},{112,144}... | collective-permute-start | bytes 129032
  326.2 1.9 collective-permute-start.7
  328.1 0.3 convolution_convert_fusion.3
  328.5 6.1 %collective-permute-start.2 = (f32[24,448]{1,0:T(8,128)S(1)}, f32[24,448]{1,0:T(8,128)S(1)}, u32[]{:S(2)}, u32[]{:S(2)}) collective-permute-start(f32[24,448]{1,0:T(8,128)S(1)} %fusion), channel_id=1, source_target_pairs={{0,48},{16,64},{32,80},{48,96},{64,112},{80,128},{96,144},{112,160... | collective-permute-start | bytes 129032
  334.6 2.2 collective-permute-start.3
  336.7 4.5 %collective-permute-start.4 = (f32[24,448]{1,0:T(8,128)S(1)}, f32[24,448]{1,0:T(8,128)S(1)}, u32[]{:S(2)}, u32[]{:S(2)}) collective-permute-start(f32[24,448]{1,0:T(8,128)S(1)} %fusion), channel_id=1, source_target_pairs={{0,80},{16,96},{32,112},{48,128},{64,144},{80,160},{96,176},{112,1... | collective-permute-start | bytes 129032
  341.3 2.7 collective-permute-start.5
  344.0 3.2 collective-permute-start.6
  347.5 1.0 copy.73
  348.6 0.8 copy.74
  349.4 0.9 collective-permute-done.5
  350.3 6.4 %collective-permute-done.6 = f32[24,448]{1,0:T(8,128)S(1)} collective-permute-done((f32[24,448]{1,0:T(8,128)S(1)}, f32[24,448]{1,0:T(8,128)S(1)}, u32[]{:S(2)}, u32[]{:S(2)}) %collective-permute-start.6) | collective-permute-done | bytes 43040
  356.6 1.1 concatenate.21
  357.8 0.7 multiply_subtract_fusion
  (74 shorter events, 1.8 us)
Async XLA Ops:
  7.2 253.1 %copy-start = (bf16[256,448]{0,1:T(8,128)(2,1)S(1)}, bf16[256,448]{0,1:T(8,128)(2,1)}, u32[]{:S(2)}) copy-start(bf16[256,448]{0,1:T(8,128)(2,1)} %param.12) | copy-start | bytes 688132
  9.6 9.2 %copy-start.13 = (bf16[256,1024]{1,0:T(8,128)(2,1)S(1)}, bf16[256,1024]{1,0:T(8,128)(2,1)}, u32[]{:S(2)}) copy-start(bf16[256,1024]{1,0:T(8,128)(2,1)} %param.16) | copy-start | bytes 1572868
  9.6 9.4 %copy-start.17 = (bf16[256,64]{0,1:T(8,128)(2,1)S(1)}, bf16[256,64]{0,1:T(8,128)(2,1)}, u32[]{:S(2)}) copy-start(bf16[256,64]{0,1:T(8,128)(2,1)} %param.14) | copy-start | bytes 98308
  9.6 57.0 %all-to-all-start = ((bf16[32,16,2048]{2,1,0:T(8,128)(2,1)}), bf16[32,16,2048]{2,1,0:T(8,128)(2,1)S(1)}, u32[]{:S(2)}, u32[]{:S(2)}) async-start(bf16[32,16,2048]{2,1,0:T(8,128)(2,1)} %stack.2), calls=%async_computation | async-start | bytes 4194304 | tf_op jit(solution)/shard_map/all_to_all | solution.py:90
  18.7 47.9 %copy-start.18 = (f32[512]{0:T(512)S(1)}, f32[512]{0:T(512)}, u32[]{:S(2)}) copy-start(f32[512]{0:T(512)} %param.15) | copy-start | bytes 6148
  18.8 237.8 %all-reduce.5.cloned.1.call-start = ((), (), s32[]{:S(2)}) async-start(), calls=%async_computation.1 | async-start | bytes 1179648 | tf_op jit(solution)/shard_map/psum | solution.py:151
  19.0 51.8 %copy-start.6 = (bf16[256,1024]{0,1:T(8,128)(2,1)}, bf16[256,1024]{0,1:T(8,128)(2,1)S(1)}, u32[]{:S(2)}) copy-start(bf16[256,1024]{0,1:T(8,128)(2,1)S(1)} %copy.89) | copy-start | bytes 1572868
  22.2 46.4 %copy-start.3 = (bf16[32,8,8,128]{3,2,1,0:T(8,128)(2,1)}, bf16[32,8,8,128]{3,2,1,0:T(8,128)(2,1)S(1)}, u32[]{:S(2)}) copy-start(bf16[32,8,8,128]{3,2,1,0:T(8,128)(2,1)S(1)} %copy.91) | copy-start | bytes 1572868
  23.3 1.7 copy-start.26
  23.3 1.7 copy-start.23
  25.1 44.5 %copy-start.20 = (f32[256]{0:T(256)}, f32[256]{0:T(256)S(1)}, u32[]{:S(2)}) copy-start(f32[256]{0:T(256)S(1)} %get-tuple-element.32) | copy-start | bytes 3076
  66.7 2.9 copy-start.1
  70.8 1.7 copy-start.4
  70.9 1.1 copy-start.9
  82.5 1.6 copy-start.11
  82.5 1.6 copy-start.12
  82.5 1.6 copy-start.22
  84.2 1.0 copy-start.7
  84.2 1.5 copy-start.10
  85.2 1.6 copy-start.2
  86.8 169.7 %copy-start.8 = (bf16[256,512]{1,0:T(8,128)(2,1)S(1)}, bf16[256,512]{1,0:T(8,128)(2,1)}, u32[]{:S(2)}) copy-start(bf16[256,512]{1,0:T(8,128)(2,1)} %param.13) | copy-start | bytes 786436
  86.8 169.7 %copy-start.19 = (f32[512]{0:T(512)S(1)}, f32[512]{0:T(512)}, u32[]{:S(2)}) copy-start(f32[512]{0:T(512)} %param.15) | copy-start | bytes 6148
  86.8 170.9 %copy-start.24 = (f32[256]{0:T(256)S(1)}, f32[256]{0:T(256)}, u32[]{:S(2)}) copy-start(f32[256]{0:T(256)} %copy-done.23) | copy-start | bytes 3076
  86.8 170.9 %copy-start.27 = (f32[32]{0:T(128)S(1)}, f32[32]{0:T(128)}, u32[]{:S(2)}) copy-start(f32[32]{0:T(128)} %copy-done.26) | copy-start | bytes 388
  86.8 172.1 %copy-start.21 = (f32[256]{0:T(256)S(1)}, f32[256]{0:T(256)}, u32[]{:S(2)}) copy-start(f32[256]{0:T(256)} %copy-done.20) | copy-start | bytes 3076
  86.9 172.1 %copy-start.25 = (f32[256]{0:T(256)S(1)}, f32[256]{0:T(256)}, u32[]{:S(2)}) copy-start(f32[256]{0:T(256)} %get-tuple-element.31) | copy-start | bytes 3076
  259.0 69.1 %copy-start.5 = (bf16[256,1024]{0,1:T(8,128)(2,1)S(1)}, bf16[256,1024]{0,1:T(8,128)(2,1)}, u32[]{:S(2)}) copy-start(bf16[256,1024]{0,1:T(8,128)(2,1)} %copy-done.4) | copy-start | bytes 1572868
  315.3 26.0 %collective-permute-start = (f32[24,448]{1,0:T(8,128)S(1)}, f32[24,448]{1,0:T(8,128)S(1)}, u32[]{:S(2)}, u32[]{:S(2)}) collective-permute-start(f32[24,448]{1,0:T(8,128)S(1)} %fusion), channel_id=1, source_target_pairs={{0,16},{16,32},{32,48},{48,64},{64,80},{80,96},{96,112},{112,128},... | collective-permute-start | bytes 129032
  319.5 24.5 %collective-permute-start.1 = (f32[24,448]{1,0:T(8,128)S(1)}, f32[24,448]{1,0:T(8,128)S(1)}, u32[]{:S(2)}, u32[]{:S(2)}) collective-permute-start(f32[24,448]{1,0:T(8,128)S(1)} %fusion), channel_id=1, source_target_pairs={{0,32},{16,48},{32,64},{48,80},{64,96},{80,112},{96,128},{112,144}... | collective-permute-start | bytes 129032
  326.2 10.6 %collective-permute-start.7 = (f32[18,448]{1,0:T(8,128)S(1)}, f32[18,448]{1,0:T(8,128)S(1)}, u32[]{:S(2)}, u32[]{:S(2)}) collective-permute-start(f32[18,448]{1,0:T(8,128)S(1)} %slice.32), channel_id=1, source_target_pairs={{0,128},{16,144},{32,160},{48,176},{64,192},{80,208},{96,224},{112... | collective-permute-start | bytes 96776
  328.4 29.3 %copy-start.14 = (f32[18,448]{1,0:T(8,128)S(1)}, f32[18,448]{1,0:T(8,128)}, u32[]{:S(2)}) copy-start(f32[18,448]{1,0:T(8,128)} %param.21) | copy-start | bytes 96772
  328.4 29.3 %copy-start.15 = (f32[18,448]{1,0:T(8,128)S(1)}, f32[18,448]{1,0:T(8,128)}, u32[]{:S(2)}) copy-start(f32[18,448]{1,0:T(8,128)} %param.22) | copy-start | bytes 96772
  328.5 29.3 %copy-start.16 = (f32[18,448]{1,0:T(8,128)S(1)}, f32[18,448]{1,0:T(8,128)}, u32[]{:S(2)}) copy-start(f32[18,448]{1,0:T(8,128)} %param.23) | copy-start | bytes 96772
  328.5 20.9 %collective-permute-start.2 = (f32[24,448]{1,0:T(8,128)S(1)}, f32[24,448]{1,0:T(8,128)S(1)}, u32[]{:S(2)}, u32[]{:S(2)}) collective-permute-start(f32[24,448]{1,0:T(8,128)S(1)} %fusion), channel_id=1, source_target_pairs={{0,48},{16,64},{32,80},{48,96},{64,112},{80,128},{96,144},{112,160... | collective-permute-start | bytes 129032
  334.6 14.8 %collective-permute-start.3 = (f32[24,448]{1,0:T(8,128)S(1)}, f32[24,448]{1,0:T(8,128)S(1)}, u32[]{:S(2)}, u32[]{:S(2)}) collective-permute-start(f32[24,448]{1,0:T(8,128)S(1)} %fusion), channel_id=1, source_target_pairs={{0,64},{16,80},{32,96},{48,112},{64,128},{80,144},{96,160},{112,17... | collective-permute-start | bytes 129032
  336.7 12.7 %collective-permute-start.4 = (f32[24,448]{1,0:T(8,128)S(1)}, f32[24,448]{1,0:T(8,128)S(1)}, u32[]{:S(2)}, u32[]{:S(2)}) collective-permute-start(f32[24,448]{1,0:T(8,128)S(1)} %fusion), channel_id=1, source_target_pairs={{0,80},{16,96},{32,112},{48,128},{64,144},{80,160},{96,176},{112,1... | collective-permute-start | bytes 129032
  341.3 9.0 %collective-permute-start.5 = (f32[24,448]{1,0:T(8,128)S(1)}, f32[24,448]{1,0:T(8,128)S(1)}, u32[]{:S(2)}, u32[]{:S(2)}) collective-permute-start(f32[24,448]{1,0:T(8,128)S(1)} %fusion), channel_id=1, source_target_pairs={{0,96},{16,112},{32,128},{48,144},{64,160},{80,176},{96,192},{112,... | collective-permute-start | bytes 129032
  344.0 12.6 %collective-permute-start.6 = (f32[24,448]{1,0:T(8,128)S(1)}, f32[24,448]{1,0:T(8,128)S(1)}, u32[]{:S(2)}, u32[]{:S(2)}) collective-permute-start(f32[24,448]{1,0:T(8,128)S(1)} %fusion), channel_id=1, source_target_pairs={{0,112},{16,128},{32,144},{48,160},{64,176},{80,192},{96,208},{112... | collective-permute-start | bytes 129032
Sparse Core Ops, SparseCore 0:
  88.6 167.9 all-reduce.4
